TPU v7x, 32 devices: a whole 2x2x4 slice. The times are simulated.
32 devices in a mesh: member: 2 (over x), tile: 16 (over z, y, core).
Axes of the slice: x: 2, y: 2, z: 4, core: 2. Of those that a mesh axis runs over, the one named last changes fastest.
Arguments:
- precip: float32 [1024, 128], P(('member', 'tile')), parts along dimension 0, may hold values from 0.2 to 2
- pet: float32 [1024, 128], P(('member', 'tile')), parts along dimension 0, may hold values from 0.05 to 0.5
- soil_init: float32 [1024, 128], P(('member', 'tile')), parts along dimension 0, may hold values from 0.05 to 0.4
- ksat: float32 [1024, 128], P(('member', 'tile')), parts along dimension 0, may hold values from 0.5 to 3
- land_mask: int32 [1024, 128], P(('member', 'tile')), parts along dimension 0, may hold values 0 or 1
- head_init: float32 [1024, 2048], P(('member', 'tile')), parts along dimension 0, may hold values from 0.2 to 2
- subsurface_init: float32 [1024, 2048], P(('member', 'tile')), parts along dimension 0, may hold values from 0.2 to 2
- conduct: float32 [1024, 2048], P(('member', 'tile')), parts along dimension 0, may hold values from 0.22 to 0.47
- drain_rate: float32 [1024, 2048], P(('member', 'tile')), parts along dimension 0, may hold values from 0.05 to 0.4
- flow_code: int32 [1024, 2048], P(('member', 'tile')), parts along dimension 0, may hold values from 0 to 3
- channel_share: float32 [1024, 2048], P(('member', 'tile')), parts along dimension 0, may hold values from 0.02 to 0.2
- cell_slot: int32 [1024, 2048], P(('member', 'tile')), parts along dimension 0, may hold values from 0 to 1023
- slot_reach: int32 [32768], P(('member', 'tile')), parts along dimension 0, may hold values from 0 to 1023
Outputs:
- soil: float32 [1024, 128], P(('member', 'tile')), parts along dimension 0
- head: float32 [1024, 2048], P(('member', 'tile')), parts along dimension 0
- subsurface: float32 [1024, 2048], P(('member', 'tile')), parts along dimension 0
- reach_inflow: float32 [32768], P(('member', 'tile')), parts along dimension 0
There are 2 independent parts, one for each index of `member`. A program takes and returns all parts, laid end to end along the dimension named above; each array names one. Nothing has to cross between parts.
Inputs may be any that keep to these rules, and one draw needn't show every extreme that they name: `slot_reach`: slot k of a tile holds a reach owned by tile index k // 64.
All inputs are finite; a program needn't handle non-finite values. No bound on the sum of `land_mask` on one device may be relied on, other than what follows from the above.
Results may differ from a plain program's by a relative error of at most 0.00002.
Values sent between devices are 32-bit elements; how exact they have to be, the bound alone decides.
A program may use at most 64 MiB of HBM per device.

v0:
```python
import functools

import jax
import jax.numpy as jnp
from jax import lax
from jax.experimental import pallas as pl
from jax.experimental.pallas import tpu as pltpu
from jax.sharding import PartitionSpec as P

ITERS = 6
HALO = 8
LANES = 128
MESH = pl.DeviceIdType.MESH
NT = (((1,), (1,)), ((), ()))


def parts_of(x, count):
    parts = []
    for _ in range(count):
        part = x.astype(jnp.bfloat16)
        parts.append(part)
        x = x - part.astype(jnp.float32)
    return parts


def kernel(
    n,
    precip,
    pet,
    soil_init,
    ksat,
    land_mask,
    head_init,
    subsurface_init,
    conduct,
    drain_rate,
    flow_code,
    channel_share,
    cell_slot,
    slot_reach,
    soil_out,
    head_out,
    sub_out,
    reach_out,
    land_in,
    mask_in,
    soil_v,
    pack,
    land_send,
    land_recv,
    wide,
    h,
    s,
    g,
    d,
    code,
    keep_h,
    keep_s,
    from_up,
    from_down,
    from_left,
    from_right,
    share_v,
    slot_v,
    inflow,
    head_v,
    sums_send,
    sums_recv,
    places,
    spots,
    reach_v,
    land_sem,
    own_sem,
    halo_send,
    halo_recv,
    a2a_send,
    a2a_recv,
    out_sem,
):
    me = lax.axis_index("tile")
    cols, land_rows = precip.shape
    rows, width = head_init.shape
    full = rows + 2 * HALO
    chunks = width // LANES
    land_dev = land_rows // n
    per_chunk = LANES // (width // n)
    per_owner = slot_reach.shape[0] * LANES // n
    twins = LANES // per_owner
    reach_rows = reach_v.shape[0]

    barrier = pltpu.get_barrier_semaphore()
    for k in range(1, n):
        pl.semaphore_signal(
            barrier, inc=1, device_id={"tile": lax.rem(me + k, n)}, device_id_type=MESH
        )

    land_copies = [
        pltpu.make_async_copy(ref, land_in.at[i], land_sem.at[i])
        for i, ref in enumerate((precip, pet, soil_init, ksat))
    ]
    land_copies.append(pltpu.make_async_copy(land_mask, mask_in, land_sem.at[4]))
    for copy in land_copies:
        copy.start()
    fields = ((head_init, h), (subsurface_init, s), (conduct, g), (drain_rate, d), (flow_code, code))
    own = [
        pltpu.make_async_copy(src, dst.at[pl.ds(HALO, rows)], own_sem.at[i])
        for i, (src, dst) in enumerate(fields)
    ]
    own.append(pltpu.make_async_copy(channel_share, share_v, own_sem.at[5]))
    own.append(pltpu.make_async_copy(cell_slot, slot_v, own_sem.at[6]))
    own.append(pltpu.make_async_copy(slot_reach.at[me // twins], places.at[me], own_sem.at[7]))
    for copy in own:
        copy.start()

    @pl.when(me == 0)
    def _():
        for _, dst in fields:
            dst[:HALO, :] = jnp.zeros((HALO, width), dst.dtype)

    @pl.when(me == n - 1)
    def _():
        for _, dst in fields:
            dst[full - HALO :, :] = jnp.zeros((HALO, width), dst.dtype)

    for copy in land_copies:
        copy.wait()
    rain, demand, water, conductivity = land_in[0], land_in[1], land_in[2], land_in[3]
    mask = mask_in[...].astype(jnp.float32)
    wet = 2.0 * water
    cap = conductivity * (1.0 - wet)
    runoff = mask * rain * rain / (rain + cap)
    drainage = 0.25 * mask * conductivity * (wet * wet) * (wet * wet)
    evap = mask * demand * wet
    soil_v[...] = water + 0.1 * (mask * rain - runoff - drainage - evap)
    soil_copy = pltpu.make_async_copy(soil_v, soil_out, out_sem.at[0])
    soil_copy.start()
    lane = lax.broadcasted_iota(jnp.int32, (cols, land_rows), 1)
    place = lax.rem(lane, land_dev)
    side = HALO // 4
    if 4 * cols < LANES:
        pack[4 * cols :, :] = jnp.zeros((LANES - 4 * cols, land_rows), jnp.float32)
    for i, x in enumerate((runoff, drainage)):
        pack[i * cols : (i + 1) * cols, :] = x
        before = jnp.where(lane >= land_dev, pltpu.roll(x, side, 1), 0.0)
        after = jnp.where(
            lane < land_rows - land_dev, pltpu.roll(x, land_rows - (land_dev - side), 1), 0.0
        )
        pack[(2 + i) * cols : (3 + i) * cols, :] = jnp.where(place < side, before, after)
    land_send[...] = jnp.transpose(pack[...]).reshape(n, land_dev, LANES)

    pl.semaphore_wait(barrier, n - 1)
    sent = []
    for k in range(1, n):
        peer = lax.rem(me + k, n)
        copy = pltpu.make_async_remote_copy(
            src_ref=land_send.at[peer],
            dst_ref=land_recv.at[lax.rem(me, per_chunk), me // per_chunk],
            send_sem=a2a_send.at[0, k],
            recv_sem=a2a_recv.at[0, k],
            device_id={"tile": peer},
            device_id_type=MESH,
        )
        copy.start()
        sent.append(copy)

    def halo_copy(i, up):
        src, dst = fields[i]
        if up:
            start, land, peer = (rows - HALO, 0, me + 1)
        else:
            start, land, peer = (0, full - HALO, me - 1)
        return pltpu.make_async_remote_copy(
            src_ref=src.at[pl.ds(start, HALO)],
            dst_ref=dst.at[pl.ds(land, HALO)],
            send_sem=halo_send.at[0 if up else 1, i],
            recv_sem=halo_recv.at[0 if up else 1, i],
            device_id={"tile": lax.rem(peer + n, n)},
            device_id_type=MESH,
        )

    @pl.when(me < n - 1)
    def _():
        for i in range(len(fields)):
            halo_copy(i, True).start()

    @pl.when(me > 0)
    def _():
        for i in range(len(fields)):
            halo_copy(i, False).start()

    for k in range(1, n):
        peer = lax.rem(me + k, n)
        copy = pltpu.make_async_remote_copy(
            src_ref=slot_reach.at[peer // twins],
            dst_ref=places.at[me],
            send_sem=a2a_send.at[1, k],
            recv_sem=a2a_recv.at[1, k],
            device_id={"tile": peer},
            device_id_type=MESH,
        )
        copy.start()
        sent.append(copy)

    land_recv[lax.rem(me, per_chunk), me // per_chunk] = land_send[me]
    for copy in sent[: n - 1]:
        copy.wait()

    l_iota = lax.broadcasted_iota(jnp.int32, (LANES, 4 * LANES), 0)
    f_iota = lax.broadcasted_iota(jnp.int32, (LANES, 4 * LANES), 1)
    cell = lax.rem(f_iota, LANES) // 4
    group = f_iota // LANES
    total = None
    for k in range(per_chunk):
        inside = (cell >= k * cols) & (cell < (k + 1) * cols)
        spread = inside & (l_iota == group * cols + cell - k * cols)
        spread = jnp.where(spread, 1.0, 0.0).astype(jnp.bfloat16)
        block = land_recv[k].reshape(chunks * land_dev, LANES)
        for part in parts_of(block, 3):
            term = jnp.dot(part, spread, preferred_element_type=jnp.float32)
            total = term if total is None else total + term
    wide[...] = total

    for copy in own:
        copy.wait()

    @pl.when(me > 0)
    def _():
        for i in range(len(fields)):
            halo_copy(i, True).wait_recv()

    @pl.when(me < n - 1)
    def _():
        for i in range(len(fields)):
            halo_copy(i, False).wait_recv()

    row8 = lax.broadcasted_iota(jnp.int32, (8, LANES), 0)
    first = lax.broadcasted_iota(jnp.int32, (full, LANES), 1) == 0
    last = lax.broadcasted_iota(jnp.int32, (full, LANES), 1) == LANES - 1
    zero = jnp.zeros((full, LANES), jnp.float32)

    def at(c):
        return pl.ds(c * LANES, LANES)

    def above(x):
        return pltpu.roll(x, 1, 0)

    def below(x):
        return pltpu.roll(x, full - 1, 0)

    def rolled(x):
        return (pltpu.roll(x, 1, 1), pltpu.roll(x, LANES - 1, 1))

    def covering(c, i):
        base = c * land_dev
        picks = [((2 + i) * LANES, r) for r in range(side)]
        picks += [(i * LANES, r) for r in range(land_dev)]
        picks += [((2 + i) * LANES, side + r) for r in range(side)]
        groups = []
        for m in range(full // 8):
            pair = []
            for lanes, r in picks[2 * m : 2 * m + 2]:
                one = wide[base + r : base + r + 1, lanes : lanes + LANES]
                pair.append(jnp.broadcast_to(one, (8, LANES)))
            groups.append(jnp.where(row8 < 4, pair[0], pair[1]))
        return jnp.concatenate(groups, axis=0)

    def load_static(c):
        gc = g[:, at(c)]
        dc = d[:, at(c)]
        kc = code[:, at(c)]
        right = jnp.where(kc == 2, dc, 0.0)
        left = jnp.where(kc == 3, dc, 0.0)
        down = jnp.where(kc == 0, dc, 0.0)
        up = jnp.where(kc == 1, dc, 0.0)
        g_r, g_l = rolled(gc)
        return gc, down, up, right, left, g_r, g_l, pltpu.roll(right, 1, 1), pltpu.roll(left, LANES - 1, 1)

    previous = None
    current = load_static(0)
    for c in range(chunks):
        following = load_static(c + 1) if c + 1 < chunks else None
        gc, down, up, right, left, g_r, g_l, r_r, l_l = current
        g_left = jnp.where(first, zero if previous is None else previous[5], g_r)
        g_right = jnp.where(last, zero if following is None else following[6], g_l)
        around = above(gc) + below(gc) + g_left + g_right
        keep_h[:, at(c)] = 1.0 - gc * around
        keep_s[:, at(c)] = 1.0 - (down + up + right + left)
        from_up[:, at(c)] = above(down)
        from_down[:, at(c)] = below(up)
        from_left[:, at(c)] = jnp.where(first, zero if previous is None else previous[7], r_r)
        from_right[:, at(c)] = jnp.where(last, zero if following is None else following[8], l_l)
        h[:, at(c)] = h[:, at(c)] + covering(c, 0)
        s[:, at(c)] = s[:, at(c)] + covering(c, 1)
        previous, current = current, following

    def load_state(c):
        hc = h[:, at(c)]
        sc = s[:, at(c)]
        gc = g[:, at(c)]
        pc = gc * hc
        return (hc, sc, gc, pc) + rolled(pc) + rolled(sc)

    def substep(_, carry):
        previous = None
        current = load_state(0)
        for c in range(chunks):
            following = load_state(c + 1) if c + 1 < chunks else None
            hc, sc, gc, pc, p_r, p_l, s_r, s_l = current
            p_left = jnp.where(first, zero if previous is None else previous[4], p_r)
            p_right = jnp.where(last, zero if following is None else following[5], p_l)
            s_left = jnp.where(first, zero if previous is None else previous[6], s_r)
            s_right = jnp.where(last, zero if following is None else following[7], s_l)
            flux = (above(pc) + below(pc)) + (p_left + p_right)
            h[:, at(c)] = keep_h[:, at(c)] * hc + gc * flux
            moved = from_up[:, at(c)] * above(sc) + from_down[:, at(c)] * below(sc)
            moved = moved + from_left[:, at(c)] * s_left + from_right[:, at(c)] * s_right
            s[:, at(c)] = keep_s[:, at(c)] * sc + moved
            previous, current = current, following
        return carry

    lax.fori_loop(0, ITERS, substep, 0)

    sub_copy = pltpu.make_async_copy(s.at[pl.ds(HALO, rows)], sub_out, out_sem.at[1])
    sub_copy.start()
    water_now = h[HALO : HALO + rows, :]
    taken = share_v[...] * water_now
    inflow[...] = taken
    head_v[...] = water_now - taken
    head_copy = pltpu.make_async_copy(head_v, head_out, out_sem.at[2])
    head_copy.start()

    owner_line = lax.broadcasted_iota(jnp.int32, (n, width), 0)
    place_line = lax.broadcasted_iota(jnp.int32, (per_owner, width), 0)

    def add_row(r, total):
        value = inflow[pl.ds(r, 1), :]
        slot = slot_v[pl.ds(r, 1), :]
        owner = slot // per_owner
        spot = slot - owner * per_owner
        left = jnp.where(owner_line == owner, value, 0.0)
        left = jnp.concatenate(parts_of(left, 2), axis=0)
        right = jnp.where(place_line == spot, 1.0, 0.0).astype(jnp.bfloat16)
        return total + lax.dot_general(left, right, NT, preferred_element_type=jnp.float32)

    total = lax.fori_loop(0, rows, add_row, jnp.zeros((2 * n, per_owner), jnp.float32))
    sums = total[:n] + total[n:]
    sums = jnp.concatenate([sums] * twins, axis=1)
    for k in range(n):
        sums_send[k] = sums[k : k + 1, :]
    sums_recv[me] = sums_send[me]
    last_sent = []
    for k in range(1, n):
        peer = lax.rem(me + k, n)
        copy = pltpu.make_async_remote_copy(
            src_ref=sums_send.at[peer],
            dst_ref=sums_recv.at[me],
            send_sem=a2a_send.at[2, k],
            recv_sem=a2a_recv.at[2, k],
            device_id={"tile": peer},
            device_id_type=MESH,
        )
        copy.start()
        last_sent.append(copy)

    for copy in sent[n - 1 :]:
        copy.wait()
    half = lax.broadcasted_iota(jnp.int32, (1, LANES), 1) // per_owner == lax.rem(me, twins)
    lane_line = lax.broadcasted_iota(jnp.int32, (LANES, LANES), 0)
    reach_line = lax.broadcasted_iota(jnp.int32, (reach_rows, LANES), 0)
    for j in range(n):
        there = places[j]
        low = lax.rem(there, LANES)
        spots[:, at(j)] = jnp.where(half & (lane_line == low), 1.0, 0.0).astype(jnp.bfloat16)
    for copy in last_sent:
        copy.wait()
    found = []
    for j in range(n):
        high = places[j] // LANES
        found.append(jnp.where(reach_line == high, sums_recv[j], 0.0))
    found = jnp.concatenate(parts_of(jnp.concatenate(found, axis=1), 3), axis=0)
    reach = lax.dot_general(found, spots[...], NT, preferred_element_type=jnp.float32)
    reach_v[...] = reach[:reach_rows] + reach[reach_rows : 2 * reach_rows] + reach[2 * reach_rows :]
    reach_copy = pltpu.make_async_copy(reach_v, reach_out, out_sem.at[3])
    reach_copy.start()

    @pl.when(me < n - 1)
    def _():
        for i in range(len(fields)):
            halo_copy(i, True).wait_send()

    @pl.when(me > 0)
    def _():
        for i in range(len(fields)):
            halo_copy(i, False).wait_send()

    for copy in (soil_copy, sub_copy, head_copy, reach_copy):
        copy.wait()


def local(*args):
    n = lax.axis_size("tile")
    precip, head_init, slot_reach = args[0], args[5], args[12]
    cols, land_rows = precip.shape
    rows, width = head_init.shape
    slots = slot_reach.shape[0]
    full = rows + 2 * HALO
    land_dev = land_rows // n
    per_chunk = LANES // (width // n)
    chunks = width // LANES
    f32, i32 = jnp.float32, jnp.int32
    tall = pltpu.VMEM((full, width), f32)
    own = pltpu.VMEM((rows, width), f32)
    anywhere = pl.BlockSpec(memory_space=pl.ANY)
    soil, head, sub, reach = pl.pallas_call(
        functools.partial(kernel, n),
        out_shape=(
            jax.ShapeDtypeStruct(precip.shape, f32),
            jax.ShapeDtypeStruct(head_init.shape, f32),
            jax.ShapeDtypeStruct(head_init.shape, f32),
            jax.ShapeDtypeStruct((slots // LANES, LANES), f32),
        ),
        in_specs=[anywhere] * 13,
        out_specs=(anywhere,) * 4,
        scratch_shapes=[
            pltpu.VMEM((4, cols, land_rows), f32),
            pltpu.VMEM((cols, land_rows), i32),
            pltpu.VMEM((cols, land_rows), f32),
            pltpu.VMEM((LANES, land_rows), f32),
            pltpu.VMEM((n, land_dev, LANES), f32),
            pltpu.VMEM((per_chunk, chunks, land_dev, LANES), f32),
            pltpu.VMEM((chunks * land_dev, 4 * LANES), f32),
            tall,
            tall,
            tall,
            tall,
            pltpu.VMEM((full, width), i32),
            tall,
            tall,
            tall,
            tall,
            tall,
            tall,
            own,
            pltpu.VMEM((rows, width), i32),
            own,
            own,
            pltpu.VMEM((n, 1, LANES), f32),
            pltpu.VMEM((n, 1, LANES), f32),
            pltpu.VMEM((n, 1, LANES), i32),
            pltpu.VMEM((LANES, n * LANES), jnp.bfloat16),
            pltpu.VMEM((slots // LANES, LANES), f32),
            pltpu.SemaphoreType.DMA((5,)),
            pltpu.SemaphoreType.DMA((8,)),
            pltpu.SemaphoreType.DMA((2, 5)),
            pltpu.SemaphoreType.DMA((2, 5)),
            pltpu.SemaphoreType.DMA((3, n)),
            pltpu.SemaphoreType.DMA((3, n)),
            pltpu.SemaphoreType.DMA((4,)),
        ],
        compiler_params=pltpu.CompilerParams(collective_id=0, has_side_effects=True),
        name="step",
    )(*args[:12], slot_reach.reshape(slots // LANES, 1, LANES))
    return soil, head, sub, reach.reshape(slots)


def solution(mesh):
    grid = P(("member", "tile"), None)
    line = P(("member", "tile"))
    return jax.shard_map(
        local,
        mesh=mesh,
        in_specs=(grid,) * 12 + (line,),
        out_specs=(grid, grid, grid, line),
        check_vma=False,
    )
```

profile of v0, /device:TPU:0, one launch (start us, length us, event | category | flops | bytes accessed | tf_op | source)
XLA Modules:
  0.0 37.7 jit_solution(17641875418625161348)
XLA Ops:
  0.6 32.7 %step.1 = (f32[32,128]{1,0:T(8,128)}, f32[32,2048]{1,0:T(8,128)}, f32[32,2048]{1,0:T(8,128)}, f32[8,128]{1,0:T(8,128)}) custom-call(f32[32,128]{1,0:T(8,128)} %precip.1, f32[32,128]{1,0:T(8,128)} %pet.1, f32[32,128]{1,0:T(8,128)} %soil_init.1, f32[32,128]{1,0:T(8,128)} %ksat.1, s32[32,128]{1,0:T(8,128)} %land_mask.1, f32[32,2048]{1,0:T(8,128)} %head_init.1, ...), custom_call_target="tpu_custom_call" | custom-call | tf_op jit(solution)/shard_map/step/pallas_call | solution.py:414
  33.3 1.3 %copy.21 = f32[32,128]{1,0:T(8,128)} copy(f32[32,128]{1,0:T(8,128)} %get-tuple-element.16) | data formatting | bytes 32768
  34.6 0.0 copy-start
  34.6 1.7 %copy.22 = f32[32,2048]{1,0:T(8,128)} copy(f32[32,2048]{1,0:T(8,128)} %get-tuple-element.17) | data formatting | bytes 524288
  36.4 0.0 copy-done
  36.4 0.0 copy-start.1
  36.4 0.7 %copy.23 = f32[32,2048]{1,0:T(8,128)} copy(f32[32,2048]{1,0:T(8,128)S(1)} %copy-done) | data formatting | bytes 524288
  37.1 0.0 copy-done.1
  37.1 0.6 %copy.24 = f32[1024]{0:T(1024)} copy(f32[1024]{0:T(1024)S(1)} %bitcast.3) | data formatting | bytes 8192
Async XLA Ops:
  34.6 1.7 %copy-start = (f32[32,2048]{1,0:T(8,128)S(1)}, f32[32,2048]{1,0:T(8,128)}, u32[]{:S(2)}) copy-start(f32[32,2048]{1,0:T(8,128)} %get-tuple-element.18) | copy-start | bytes 786436
  36.4 0.7 %copy-start.1 = (f32[8,128]{1,0:T(8,128)S(1)}, f32[8,128]{1,0:T(8,128)}, u32[]{:S(2)}) copy-start(f32[8,128]{1,0:T(8,128)} %get-tuple-element.11) | copy-start | bytes 12292
where the time goes:
time: 37.9 us; the launch traced here: 37.7 us
  Pallas kernels  32.7 us (86%)
  local copies, waits for them, and re-layouts  4.34 us (11%)
  between operations  0.65 us (2%)
    pallas_call x1, Pallas kernels, local(): pl.pallas_call(functools.partial(kernel, n), out_shape=(jax.ShapeDtypeStr...  32.7 us
    unnamed x8, local copies, waits for them, and re-layouts  4.34 us

commit v1 on v0

--- a/solution.py
+++ b/solution.py
@@ -44,7 +44,6 @@
     reach_out,
     land_in,
     mask_in,
-    soil_v,
     pack,
     land_send,
     land_recv,
@@ -63,19 +62,16 @@
     share_v,
     slot_v,
     inflow,
-    head_v,
     sums_send,
     sums_recv,
     places,
     spots,
-    reach_v,
     land_sem,
     own_sem,
     halo_send,
     halo_recv,
     a2a_send,
     a2a_recv,
-    out_sem,
 ):
     me = lax.axis_index("tile")
     cols, land_rows = precip.shape
@@ -86,7 +82,7 @@
     per_chunk = LANES // (width // n)
     per_owner = slot_reach.shape[0] * LANES // n
     twins = LANES // per_owner
-    reach_rows = reach_v.shape[0]
+    reach_rows = reach_out.shape[0]
 
     barrier = pltpu.get_barrier_semaphore()
     for k in range(1, n):
@@ -131,9 +127,7 @@
     runoff = mask * rain * rain / (rain + cap)
     drainage = 0.25 * mask * conductivity * (wet * wet) * (wet * wet)
     evap = mask * demand * wet
-    soil_v[...] = water + 0.1 * (mask * rain - runoff - drainage - evap)
-    soil_copy = pltpu.make_async_copy(soil_v, soil_out, out_sem.at[0])
-    soil_copy.start()
+    soil_out[...] = water + 0.1 * (mask * rain - runoff - drainage - evap)
     lane = lax.broadcasted_iota(jnp.int32, (cols, land_rows), 1)
     place = lax.rem(lane, land_dev)
     side = HALO // 4
@@ -166,12 +160,12 @@
     def halo_copy(i, up):
         src, dst = fields[i]
         if up:
-            start, land, peer = (rows - HALO, 0, me + 1)
+            start, land, peer = (rows - ITERS, HALO - ITERS, me + 1)
         else:
             start, land, peer = (0, full - HALO, me - 1)
         return pltpu.make_async_remote_copy(
-            src_ref=src.at[pl.ds(start, HALO)],
-            dst_ref=dst.at[pl.ds(land, HALO)],
+            src_ref=src.at[pl.ds(start, ITERS)],
+            dst_ref=dst.at[pl.ds(land, ITERS)],
             send_sem=halo_send.at[0 if up else 1, i],
             recv_sem=halo_recv.at[0 if up else 1, i],
             device_id={"tile": lax.rem(peer + n, n)},
@@ -320,14 +314,11 @@
 
     lax.fori_loop(0, ITERS, substep, 0)
 
-    sub_copy = pltpu.make_async_copy(s.at[pl.ds(HALO, rows)], sub_out, out_sem.at[1])
-    sub_copy.start()
+    sub_out[...] = s[HALO : HALO + rows, :]
     water_now = h[HALO : HALO + rows, :]
     taken = share_v[...] * water_now
     inflow[...] = taken
-    head_v[...] = water_now - taken
-    head_copy = pltpu.make_async_copy(head_v, head_out, out_sem.at[2])
-    head_copy.start()
+    head_out[...] = water_now - taken
 
     owner_line = lax.broadcasted_iota(jnp.int32, (n, width), 0)
     place_line = lax.broadcasted_iota(jnp.int32, (per_owner, width), 0)
@@ -342,7 +333,7 @@
         right = jnp.where(place_line == spot, 1.0, 0.0).astype(jnp.bfloat16)
         return total + lax.dot_general(left, right, NT, preferred_element_type=jnp.float32)
 
-    total = lax.fori_loop(0, rows, add_row, jnp.zeros((2 * n, per_owner), jnp.float32))
+    total = lax.fori_loop(0, rows, add_row, jnp.zeros((2 * n, per_owner), jnp.float32), unroll=8)
     sums = total[:n] + total[n:]
     sums = jnp.concatenate([sums] * twins, axis=1)
     for k in range(n):
@@ -379,9 +370,7 @@
         found.append(jnp.where(reach_line == high, sums_recv[j], 0.0))
     found = jnp.concatenate(parts_of(jnp.concatenate(found, axis=1), 3), axis=0)
     reach = lax.dot_general(found, spots[...], NT, preferred_element_type=jnp.float32)
-    reach_v[...] = reach[:reach_rows] + reach[reach_rows : 2 * reach_rows] + reach[2 * reach_rows :]
-    reach_copy = pltpu.make_async_copy(reach_v, reach_out, out_sem.at[3])
-    reach_copy.start()
+    reach_out[...] = reach[:reach_rows] + reach[reach_rows : 2 * reach_rows] + reach[2 * reach_rows :]
 
     @pl.when(me < n - 1)
     def _():
@@ -392,9 +381,6 @@
     def _():
         for i in range(len(fields)):
             halo_copy(i, False).wait_send()
-
-    for copy in (soil_copy, sub_copy, head_copy, reach_copy):
-        copy.wait()
 
 
 def local(*args):
@@ -414,17 +400,16 @@
     soil, head, sub, reach = pl.pallas_call(
         functools.partial(kernel, n),
         out_shape=(
-            jax.ShapeDtypeStruct(precip.shape, f32),
-            jax.ShapeDtypeStruct(head_init.shape, f32),
-            jax.ShapeDtypeStruct(head_init.shape, f32),
-            jax.ShapeDtypeStruct((slots // LANES, LANES), f32),
+            pltpu.VMEM(precip.shape, f32),
+            pltpu.VMEM(head_init.shape, f32),
+            pltpu.VMEM(head_init.shape, f32),
+            pltpu.VMEM((slots // LANES, LANES), f32),
         ),
         in_specs=[anywhere] * 13,
-        out_specs=(anywhere,) * 4,
+        out_specs=(pl.BlockSpec(memory_space=pltpu.VMEM),) * 4,
         scratch_shapes=[
             pltpu.VMEM((4, cols, land_rows), f32),
             pltpu.VMEM((cols, land_rows), i32),
-            pltpu.VMEM((cols, land_rows), f32),
             pltpu.VMEM((LANES, land_rows), f32),
             pltpu.VMEM((n, land_dev, LANES), f32),
             pltpu.VMEM((per_chunk, chunks, land_dev, LANES), f32),
@@ -442,24 +427,21 @@
             tall,
             own,
             pltpu.VMEM((rows, width), i32),
-            own,
             own,
             pltpu.VMEM((n, 1, LANES), f32),
             pltpu.VMEM((n, 1, LANES), f32),
             pltpu.VMEM((n, 1, LANES), i32),
             pltpu.VMEM((LANES, n * LANES), jnp.bfloat16),
-            pltpu.VMEM((slots // LANES, LANES), f32),
             pltpu.SemaphoreType.DMA((5,)),
             pltpu.SemaphoreType.DMA((8,)),
             pltpu.SemaphoreType.DMA((2, 5)),
             pltpu.SemaphoreType.DMA((2, 5)),
             pltpu.SemaphoreType.DMA((3, n)),
             pltpu.SemaphoreType.DMA((3, n)),
-            pltpu.SemaphoreType.DMA((4,)),
         ],
-        compiler_params=pltpu.CompilerParams(collective_id=0, has_side_effects=True),
+        compiler_params=pltpu.CompilerParams(collective_id=0, has_side_effects=True, vmem_limit_bytes=16 * 2**20),
         name="step",
-    )(*args[:12], slot_reach.reshape(slots // LANES, 1, LANES))
+    )(*[pltpu.with_memory_space_constraint(x, pltpu.HBM) for x in (*args[:12], slot_reach.reshape(slots // LANES, 1, LANES))])
     return soil, head, sub, reach.reshape(slots)
 
 

time: 37.9 us -> 29.3 us (0.77)
  Pallas kernels: 32.7 us -> 25.9 us
  local copies, waits for them, and re-layouts: 4.34 us -> 2.61 us
    pallas_call x1, Pallas kernels: 32.7 us -> 25.9 us  [local(): pl.pallas_call(functools.partial(kernel, n), out_shape=(pltpu.VMEM(precip...]
    unnamed x8 -> x4, local copies, waits for them, and re-layouts: 4.34 us -> 2.61 us
where the time goes in v1:
time: 29.3 us; the launch traced here: 29.1 us
  Pallas kernels  25.9 us (88%)
  local copies, waits for them, and re-layouts  2.61 us (9%)
  between operations  0.65 us (2%)
    pallas_call x1, Pallas kernels, local(): pl.pallas_call(functools.partial(kernel, n), out_shape=(pltpu.VMEM(precip...  25.9 us
    unnamed x4, local copies, waits for them, and re-layouts  2.61 us

profile of v1, /device:TPU:0, one launch (start us, length us, event | category | flops | bytes accessed | tf_op | source)
XLA Modules:
  0.0 29.1 jit_solution(8815991455476538721)
XLA Ops:
  0.6 25.9 %step.1 = (f32[32,128]{1,0:T(8,128)S(1)}, f32[32,2048]{1,0:T(8,128)S(1)}, f32[32,2048]{1,0:T(8,128)S(1)}, f32[8,128]{1,0:T(8,128)S(1)}) custom-call(f32[32,128]{1,0:T(8,128)} %precip.1, f32[32,128]{1,0:T(8,128)} %pet.1, f32[32,128]{1,0:T(8,128)} %soil_init.1, f32[32,128]{1,0:T(8,128)} %ksat.1, s32[32,128]{1,0:T(8,128)} %land_mask.1, f32[32,2048]{1,0:T(8,128)} %head_init.1, ...), custom_call_target="tpu_custom_call" | custom-call | tf_op jit(solution)/shard_map/step/pallas_call | solution.py:400
  26.5 0.6 %copy.21 = f32[32,128]{1,0:T(8,128)} copy(f32[32,128]{1,0:T(8,128)S(1)} %get-tuple-element.12) | data formatting | bytes 32768
  27.1 0.6 %copy.24 = f32[1024]{0:T(1024)} copy(f32[1024]{0:T(1024)S(1)} %bitcast.2) | data formatting | bytes 8192
  27.7 0.7 %copy.22 = f32[32,2048]{1,0:T(8,128)} copy(f32[32,2048]{1,0:T(8,128)S(1)} %get-tuple-element.13) | data formatting | bytes 524288
  28.4 0.7 %copy.23 = f32[32,2048]{1,0:T(8,128)} copy(f32[32,2048]{1,0:T(8,128)S(1)} %get-tuple-element.14) | data formatting | bytes 524288
